TPU v7x, 256 devices: a whole 4x4x8 slice. The times are simulated.
256 devices in a mesh: gx: 16 (over z, core), gy: 16 (over y, x).
Axes of the slice: x: 4, y: 4, z: 8, core: 2. Of those that a mesh axis runs over, the one named last changes fastest.
Arguments:
- modes: float32 [524288, 512], P(('gx', 'gy'))
- batch: float32 [524288, 256], P(('gx', 'gy')), as said below
- core: float32 [768, 512], replicated, may hold values from -0.21875 to 0.21875
Outputs:
- new_modes: float32 [524288, 512], P(('gx', 'gy'))
Inputs may be any that keep to these rules, and one draw needn't show every extreme that they name: Each row of modes and batch shares one positive scale; batch holds a sizeable part of the span of modes.
All inputs are finite; a program needn't handle non-finite values.
Results may differ from a plain program's by a relative error of at most 0.000058.
Values sent between devices are 32-bit elements; how exact they have to be, the bound alone decides.
A program may use at most 64 MiB of HBM per device.

v0:
```python
import jax
import jax.numpy as jnp
from jax import lax
from jax.sharding import PartitionSpec as P


def matmul(left, right):
    return jnp.dot(left, right, precision=lax.Precision.HIGHEST, preferred_element_type=jnp.float32)


def global_sum(parts):
    return lax.psum((parts[0],), ("gx", "gy"))


def shards(modes, batch, core):
    total_rows = modes.shape[0] * lax.axis_size("gx") * lax.axis_size("gy")
    width = modes.shape[1]
    top = matmul(modes, core[:width])
    cross = global_sum((matmul(modes.T, batch),))[0]
    coeffs = cross / total_rows
    resid = batch - matmul(modes, coeffs)
    gram = global_sum((matmul(resid.T, resid),))[0] / total_rows
    lower = jnp.linalg.cholesky(gram)
    basis = jax.scipy.linalg.solve_triangular(lower, resid.T, lower=True).T
    return top + matmul(basis, core[width:])


def solution(mesh):
    placed = (P(("gx", "gy"), None), P(("gx", "gy"), None), P())
    return jax.shard_map(
        shards, mesh=mesh, in_specs=placed, out_specs=P(("gx", "gy"), None), check_vma=False
    )
```

profile of v0, /device:TPU:2, one launch (start us, length us, event | category | flops | bytes accessed | tf_op | source)
XLA Modules:
  0.0 619.7 jit_solution(16031329301337902461)
XLA Ops:
  6.5 10.5 %fusion.20 = f32[512,256]{1,0:T(8,128)} fusion(f32[2048,512]{1,0:T(8,128)} %param.3, f32[2048,256]{1,0:T(8,128)} %param.4), kind=kOutput, calls=%fused_computation.42 | convolution fusion | flops 3221225472 | bytes 6815744 | tf_op jit(solution)/shard_map/dot_general | solution.py:8
  17.0 0.0 all-reduce.4.cloned.1.call-update
  17.0 0.5 all-reduce.6.cloned.1.call-start
  17.6 1.8 copy.4
  19.4 256.1 %all-reduce.4.cloned.1.call-done = f32[512,256]{1,0:T(8,128)} async-done(((f32[512,256]{1,0:T(8,128)}), f32[512,256]{1,0:T(8,128)}) %all-reduce.4.cloned.1.call-update) | async-done | bytes 524304 | tf_op jit(solution)/shard_map/psum | solution.py:12
  275.5 9.9 %fusion = f32[2048,256]{0,1:T(8,128)S(1)} fusion(f32[2048,256]{0,1:T(8,128)} %copy.4, f32[2048,512]{1,0:T(8,128)} %param.3, f32[512,256]{1,0:T(8,128)} %all-reduce.4.cloned.1.call-done), kind=kOutput, calls=%fused_computation.4 | convolution fusion | flops 3221880832 | bytes 8912896 | tf_op jit(solution)/shard_map/dot_general | solution.py:8
  285.5 2.6 fusion.21
  288.0 0.0 all-reduce.6.cloned.1.call-update
  288.1 10.2 %fusion.6 = f32[2048,512]{1,0:T(8,128)} fusion(f32[2048,512]{1,0:T(8,128)} %param.3, f32[768,512]{1,0:T(8,128)} %param.5), kind=kOutput, calls=%fused_computation.12 | convolution fusion | flops 6442450944 | bytes 9437184 | tf_op jit(solution)/shard_map/dot_general | solution.py:8
  298.3 242.9 %all-reduce.6.cloned.1.call-done = f32[256,256]{0,1:T(8,128)} async-done(((f32[256,256]{0,1:T(8,128)}), f32[256,256]{0,1:T(8,128)}) %all-reduce.6.cloned.1.call-update) | async-done | bytes 262160 | tf_op jit(solution)/shard_map/psum | solution.py:12
  541.2 1.0 broadcast_multiply_fusion
  542.2 0.1 copy.6
  542.3 1.0 fusion.10
  543.3 11.7 %cholesky.50 = f32[128,128]{1,0:T(8,128)S(1)} custom-call(f32[128,128]{1,0:T(8,128)S(1)} %cholesky.118), custom_call_target="Cholesky" | custom-call | tf_op jit(solution)/shard_map/jit(cholesky)/cholesky | solution.py:23
  555.0 9.8 %custom-call.15 = f32[1,128,128]{1,2,0:T(8,128)S(1)} custom-call(f32[1,128,128]{2,1,0:T(8,128)S(1)} %get-tuple-element.26), custom_call_target="InvertDiagBlocksLowerTriangular" | custom-call | tf_op jit(solution)/shard_map/jit(cholesky)/cholesky | solution.py:23
  564.9 0.2 constant_dynamic-update-slice_fusion.1
  565.1 0.3 convolution_subtract_fusion.1
  565.4 11.7 %cholesky.105 = f32[128,128]{1,0:T(8,128)S(1)} custom-call(f32[128,128]{1,0:T(8,128)S(1)} %convolution_subtract_fusion.1), custom_call_target="Cholesky" | custom-call | tf_op jit(solution)/shard_map/jit(cholesky)/cholesky | solution.py:23
  577.1 0.7 compare_reduce_fusion
  579.1 0.1 triangular_solve.57
  579.2 4.1 while.1
  579.2 0.7 fusion.33
  579.9 1.3 bitcast_dynamic-update-slice_fusion.2
  581.2 0.7 fusion.33
  581.9 1.3 bitcast_dynamic-update-slice_fusion.2
  583.3 19.9 %custom-call.16 = f32[2,128,128]{1,2,0:T(8,128)S(1)} custom-call(f32[2,128,128]{2,1,0:T(8,128)S(1)} %get-tuple-element.12), custom_call_target="InvertDiagBlocksLowerTriangular" | custom-call | tf_op jit(solution)/shard_map/jit(_solve_triangular)/triangular_solve | solution.py:24
  603.2 1.1 fusion.4
  604.2 0.0 copy-start
  604.2 1.0 convolution_subtract_fusion
  605.2 1.1 fusion.13
  606.3 0.1 copy-done
  606.4 6.2 %convolution_add_fusion = f32[2048,512]{1,0:T(8,128)} fusion(f32[2048,512]{1,0:T(8,128)S(1)} %copy-done, f32[128,2048]{1,0:T(8,128)S(1)} %fusion.13, f32[128,2048]{1,0:T(8,128)S(1)} %fusion.4, f32[768,512]{1,0:T(8,128)} %param.5), kind=kOutput, calls=%fused_computation.2 | convolution fusion | flops 3222798336 | bytes 11010048 | tf_op jit(solution)/shard_map/dot_general | solution.py:8
  (12 shorter events, 0.2 us)
Async XLA Ops:
  6.5 11.0 %copy-start.1 = (f32[2048,256]{1,0:T(8,128)S(1)}, f32[2048,256]{1,0:T(8,128)}, u32[]{:S(2)}) copy-start(f32[2048,256]{1,0:T(8,128)} %param.4) | copy-start | bytes 6291460
  6.5 269.0 %all-reduce.4.cloned.1.call-start = ((), (), s32[]{:S(2)}) async-start(), calls=%async_computation | async-start | bytes 1048576 | tf_op jit(solution)/shard_map/psum | solution.py:12
  17.0 524.1 %all-reduce.6.cloned.1.call-start = ((), (), s32[]{:S(2)}) async-start(), calls=%async_computation.1 | async-start | bytes 524288 | tf_op jit(solution)/shard_map/psum | solution.py:12
  604.2 2.2 copy-start
Sparse Core Ops, SparseCore 0:
  17.2 258.3 all-reduce.3
  288.2 252.9 all-reduce.5
where the time goes:
time: 625 us; the launch traced here: 620 us
  waiting for transfers between devices  499 us (80%)
  other arithmetic  55.9 us (9%)
  matrix products  43 us (7%)
  between operations  15 us (2%)
    psum x2, waiting for transfers between devices, global_sum(): return lax.psum((parts[0],), ('gx', 'gy'))  499 us
    dot_general x5, matrix products, matmul(): jnp.dot(left, right, precision=lax.Precision.HIGHEST, preferred_element_t...  39.5 us
    another operation x6, other arithmetic, shards(): lower = jnp.linalg.cholesky(gram)  34 us
    another operation x3, other arithmetic, shards(): basis = jax.scipy.linalg.solve_triangular(lower, resid.T, lower=True).T  19.9 us
  transfers between devices with their start and end apart: 2, of which 2 were waited for; matrix products, arithmetic and copies ran while one was open for 2% of the time, Pallas kernels for 0%

commit v1 on v0

--- a/solution.py
+++ b/solution.py
@@ -9,7 +9,7 @@
 
 
 def global_sum(parts):
-    return lax.psum((parts[0],), ("gx", "gy"))
+    return lax.psum(lax.psum((parts[0],), axis_name="gy"), axis_name="gx")
 
 
 def shards(modes, batch, core):

time: 625 us -> 532 us (0.85)
  waiting for transfers between devices: 499 us -> 406 us
    psum x2 -> x4, waiting for transfers between devices: 499 us -> 406 us  [global_sum(): return lax.psum(lax.psum((parts[0],), axis_name='gy'), axis_name='gx')]
  transfers between devices with their start and end apart: 2 -> 4, of which waited for: 2 -> 4; matrix products, arithmetic and copies ran while one was open for 2% -> 2% of each run, Pallas kernels for 0% -> 0%
where the time goes in v1:
time: 532 us; the launch traced here: 526 us
  waiting for transfers between devices  406 us (76%)
  other arithmetic  55.9 us (11%)
  matrix products  43 us (8%)
  between operations  14.8 us (3%)
  local copies, waits for them, and re-layouts  6.17 us (1%)
    psum x4, waiting for transfers between devices, global_sum(): return lax.psum(lax.psum((parts[0],), axis_name='gy'), axis_name='gx')  406 us
    dot_general x5, matrix products, matmul(): jnp.dot(left, right, precision=lax.Precision.HIGHEST, preferred_element_t...  39.4 us
    another operation x6, other arithmetic, shards(): lower = jnp.linalg.cholesky(gram)  34 us
    another operation x3, other arithmetic, shards(): basis = jax.scipy.linalg.solve_triangular(lower, resid.T, lower=True).T  19.9 us
  transfers between devices with their start and end apart: 4, of which 4 were waited for; matrix products, arithmetic and copies ran while one was open for 2% of the time, Pallas kernels for 0%

profile of v1, /device:TPU:2, one launch (start us, length us, event | category | flops | bytes accessed | tf_op | source)
XLA Modules:
  0.0 526.3 jit_solution(12167794753438697266)
XLA Ops:
  6.5 10.5 %fusion.20 = f32[512,256]{1,0:T(8,128)} fusion(f32[2048,512]{1,0:T(8,128)} %param.3, f32[2048,256]{1,0:T(8,128)} %param.4), kind=kOutput, calls=%fused_computation.42 | convolution fusion | flops 3221225472 | bytes 6815744 | tf_op jit(solution)/shard_map/dot_general | solution.py:8
  17.1 98.5 %all-reduce.6.cloned.1.call-done = f32[512,256]{1,0:T(8,128)} async-done(((f32[512,256]{1,0:T(8,128)}), f32[512,256]{1,0:T(8,128)}) %all-reduce.6.cloned.1.call-update) | async-done | bytes 524304 | tf_op jit(solution)/shard_map/psum | solution.py:12
  115.6 0.5 all-reduce.10.cloned.1.call-start
  116.1 1.8 copy.4
  117.9 110.4 %all-reduce.8.cloned.1.call-done = f32[512,256]{1,0:T(8,128)} async-done(((f32[512,256]{1,0:T(8,128)}), f32[512,256]{1,0:T(8,128)}) %all-reduce.8.cloned.1.call-update) | async-done | bytes 524304 | tf_op jit(solution)/shard_map/psum | solution.py:12
  228.3 9.9 %fusion = f32[2048,256]{0,1:T(8,128)S(1)} fusion(f32[2048,256]{0,1:T(8,128)} %copy.4, f32[2048,512]{1,0:T(8,128)} %param.3, f32[512,256]{1,0:T(8,128)} %all-reduce.8.cloned.1.call-done), kind=kOutput, calls=%fused_computation.4 | convolution fusion | flops 3221880832 | bytes 8912896 | tf_op jit(solution)/shard_map/dot_general | solution.py:8
  238.3 2.6 fusion.21
  240.9 0.0 all-reduce.12.cloned.1.call-start
  240.9 95.2 %all-reduce.10.cloned.1.call-done = f32[256,256]{0,1:T(8,128)} async-done(((f32[256,256]{0,1:T(8,128)}), f32[256,256]{0,1:T(8,128)}) %all-reduce.10.cloned.1.call-update) | async-done | bytes 262160 | tf_op jit(solution)/shard_map/psum | solution.py:12
  336.1 10.2 %fusion.6 = f32[2048,512]{1,0:T(8,128)} fusion(f32[2048,512]{1,0:T(8,128)} %param.3, f32[768,512]{1,0:T(8,128)} %param.5), kind=kOutput, calls=%fused_computation.12 | convolution fusion | flops 6442450944 | bytes 9437184 | tf_op jit(solution)/shard_map/dot_general | solution.py:8
  346.4 101.7 %all-reduce.12.cloned.1.call-done = f32[256,256]{0,1:T(8,128)} async-done(((f32[256,256]{0,1:T(8,128)}), f32[256,256]{0,1:T(8,128)}) %all-reduce.12.cloned.1.call-update) | async-done | bytes 262160 | tf_op jit(solution)/shard_map/psum | solution.py:12
  448.1 1.0 broadcast_multiply_fusion
  449.0 0.1 copy.6
  449.2 1.0 fusion.10
  450.2 11.7 %cholesky.50 = f32[128,128]{1,0:T(8,128)S(1)} custom-call(f32[128,128]{1,0:T(8,128)S(1)} %cholesky.118), custom_call_target="Cholesky" | custom-call | tf_op jit(solution)/shard_map/jit(cholesky)/cholesky | solution.py:23
  461.9 9.8 %custom-call.15 = f32[1,128,128]{1,2,0:T(8,128)S(1)} custom-call(f32[1,128,128]{2,1,0:T(8,128)S(1)} %get-tuple-element.26), custom_call_target="InvertDiagBlocksLowerTriangular" | custom-call | tf_op jit(solution)/shard_map/jit(cholesky)/cholesky | solution.py:23
  471.8 0.2 constant_dynamic-update-slice_fusion.1
  472.0 0.3 convolution_subtract_fusion.1
  472.2 11.7 %cholesky.105 = f32[128,128]{1,0:T(8,128)S(1)} custom-call(f32[128,128]{1,0:T(8,128)S(1)} %convolution_subtract_fusion.1), custom_call_target="Cholesky" | custom-call | tf_op jit(solution)/shard_map/jit(cholesky)/cholesky | solution.py:23
  484.0 0.7 compare_reduce_fusion
  486.0 0.1 triangular_solve.57
  486.1 4.1 while.1
  486.1 0.7 fusion.33
  486.8 1.3 bitcast_dynamic-update-slice_fusion.2
  488.1 0.7 fusion.33
  488.8 1.3 bitcast_dynamic-update-slice_fusion.2
  490.1 19.9 %custom-call.16 = f32[2,128,128]{1,2,0:T(8,128)S(1)} custom-call(f32[2,128,128]{2,1,0:T(8,128)S(1)} %get-tuple-element.12), custom_call_target="InvertDiagBlocksLowerTriangular" | custom-call | tf_op jit(solution)/shard_map/jit(_solve_triangular)/triangular_solve | solution.py:24
  510.0 1.1 fusion.4
  511.1 1.0 convolution_subtract_fusion
  512.1 1.1 fusion.13
  513.2 0.1 copy-done
  513.3 6.2 %convolution_add_fusion = f32[2048,512]{1,0:T(8,128)} fusion(f32[2048,512]{1,0:T(8,128)S(1)} %copy-done, f32[128,2048]{1,0:T(8,128)S(1)} %fusion.13, f32[128,2048]{1,0:T(8,128)S(1)} %fusion.4, f32[768,512]{1,0:T(8,128)} %param.5), kind=kOutput, calls=%fused_computation.2 | convolution fusion | flops 3222798336 | bytes 11010048 | tf_op jit(solution)/shard_map/dot_general | solution.py:8
  (18 shorter events, 0.3 us)
Async XLA Ops:
  6.5 109.1 %all-reduce.6.cloned.1.call-start = ((), (), s32[]{:S(2)}) async-start(), calls=%async_computation | async-start | bytes 1048576 | tf_op jit(solution)/shard_map/psum | solution.py:12
  6.5 109.6 %copy-start.1 = (f32[2048,256]{1,0:T(8,128)S(1)}, f32[2048,256]{1,0:T(8,128)}, u32[]{:S(2)}) copy-start(f32[2048,256]{1,0:T(8,128)} %param.4) | copy-start | bytes 6291460
  17.0 211.3 %all-reduce.8.cloned.1.call-start = ((), (), s32[]{:S(2)}) async-start(), calls=%async_computation.1 | async-start | bytes 1048576 | tf_op jit(solution)/shard_map/psum | solution.py:12
  115.6 220.5 %all-reduce.10.cloned.1.call-start = ((), (), s32[]{:S(2)}) async-start(), calls=%async_computation.2 | async-start | bytes 524288 | tf_op jit(solution)/shard_map/psum | solution.py:12
  240.9 207.2 %all-reduce.12.cloned.1.call-start = ((), (), s32[]{:S(2)}) async-start(), calls=%async_computation.3 | async-start | bytes 524288 | tf_op jit(solution)/shard_map/psum | solution.py:12
  511.1 2.2 copy-start
Sparse Core Ops, SparseCore 0:
  17.1 98.4 all-reduce.5
  117.9 110.3 all-reduce.7
  241.0 95.0 all-reduce.9
  338.3 109.7 all-reduce.11
